TPU v7x, 512 devices: a whole 4x8x8 slice. The times are simulated.
512 devices in a mesh: dom: 128 (over y, z, core), scen: 4 (over x).
Axes of the slice: x: 4, y: 8, z: 8, core: 2. Of those that a mesh axis runs over, the one named last changes fastest.
Arguments:
- embedding: bfloat16 [1310720, 256], P(('dom', 'scen')), may hold values from -6 to 6
- scenario_feats: bfloat16 [16, 1310720], P(None, ('dom', 'scen')), may hold values from -6 to 6
- adjacency: bfloat16 [10240, 2, 128, 128], P(('dom', 'scen')), may hold values from -0.3125 to 0.3125
- driver_weight: bfloat16 [1310720, 128], P(('dom', 'scen')), may hold values from -0.3125 to 0.3125
- local_slot: int32 [10240], P(('dom', 'scen')), may hold values from 0 to 79, as said below
- halo_slot: int32 [10240], P(('dom', 'scen')), may hold values from 0 to 15, as said below
- send_rows: int32 [65536, 16], P(('dom', 'scen')), may hold values from 0 to 2559
- send_count: int32 [65536], P(('dom', 'scen')), may hold values from 1 to 16, as said below
- hot_ids: int32 [128], replicated, may hold values from 0 to 1310719, as said below
- first_weight: bfloat16 [512, 256], P('scen'), may hold values from -0.25 to 0.25
- feature_weight: bfloat16 [16, 256], replicated, may hold values from -1.5 to 1.5
- first_bias: float32 [256], replicated, may hold values from -3 to 3
- second_weight: bfloat16 [256, 256], P('scen'), may hold values from -0.375 to 0.375
- second_bias: float32 [256], replicated, may hold values from -3 to 3
Outputs:
- updated: bfloat16 [1310720, 256], P(('dom', 'scen'))
Inputs may be any that keep to these rules, and one draw needn't show every extreme that they name: `local_slot`: the 20 entries of one device are distinct and name exactly 5 tiles of each device of its partition; values s * 20 to s * 20 + 19 are tiles of scen index s. `halo_slot`: the entries of one device name every halo tile at least once. `send_count`: every device has a partition to which it sends 16 pins. `hot_ids`: no device holds more than 1 of them, and some device holds exactly that many.
All inputs are finite; a program needn't handle non-finite values.
Results may differ from a plain program's by a relative error of at most 0.0038.
Values may be sent and summed in bfloat16 or wider, within the bound.
No kernel may reach another device: no remote copies, remote signals or barrier semaphores. Data moves between devices by JAX's collectives and lax.ppermute only.
A program may use at most 64 MiB of HBM per device.

v0:
```python
import jax
import jax.numpy as jnp
from jax import lax
from jax.sharding import PartitionSpec as P


def per_device(
    embedding,
    scenario_feats,
    adjacency,
    driver_weight,
    local_slot,
    halo_slot,
    send_rows,
    send_count,
    hot_ids,
    first_weight,
    feature_weight,
    first_bias,
    second_weight,
    second_bias,
):
    rows, width = embedding.shape
    tile = adjacency.shape[-1]
    tiles = rows // tile
    groups = lax.axis_size("scen")
    partition = lax.all_gather(embedding, "scen", axis=0, tiled=True)
    local_tiles = partition.reshape(groups * tiles, tile, width)[local_slot]
    slots_per_peer = send_rows.shape[1]
    live = jnp.arange(slots_per_peer, dtype=jnp.int32)[None, :] < send_count[:, None]
    outgoing_rows = jnp.where(
        live[:, :, None], embedding[send_rows], jnp.zeros((), embedding.dtype)
    )
    incoming = lax.all_to_all(outgoing_rows, "dom", split_axis=0, concat_axis=0, tiled=True)
    halo_tiles = incoming.reshape(-1, tile, width)[halo_slot]
    myself = lax.axis_index(("dom", "scen"))
    owner = hot_ids // rows
    within = hot_ids - owner * rows
    mine = jnp.where(
        (owner == myself)[:, None], embedding[within].astype(jnp.float32), jnp.float32(0.0)
    )
    drivers = lax.psum(mine, ("dom", "scen")).astype(jnp.bfloat16)
    summed = jnp.einsum(
        "tij,tjc->tic", adjacency[:, 0], local_tiles, preferred_element_type=jnp.float32
    )
    summed = summed + jnp.einsum(
        "tij,tjc->tic", adjacency[:, 1], halo_tiles, preferred_element_type=jnp.float32
    )
    summed = summed.reshape(rows, width) + jnp.dot(
        driver_weight, drivers, preferred_element_type=jnp.float32
    )
    aggregate = summed.astype(jnp.bfloat16)
    joined = jnp.concatenate([embedding, aggregate], axis=1)
    starting = (
        jnp.dot(scenario_feats.T, feature_weight, preferred_element_type=jnp.float32) + first_bias
    )
    columns = joined
    inner = starting + jnp.dot(
        columns,
        lax.all_gather(first_weight, "scen", axis=0, tiled=True),
        preferred_element_type=jnp.float32,
    )
    activated = jax.nn.gelu(inner, approximate=False).astype(jnp.bfloat16)
    residual = embedding.astype(jnp.float32) + second_bias
    columns = activated
    result = residual + jnp.dot(
        columns,
        lax.all_gather(second_weight, "scen", axis=0, tiled=True),
        preferred_element_type=jnp.float32,
    )
    return result.astype(jnp.bfloat16)


def solution(mesh):
    return jax.shard_map(
        per_device,
        mesh=mesh,
        in_specs=(
            P(("dom", "scen"), None),
            P(None, ("dom", "scen")),
            P(("dom", "scen"), None, None, None),
            P(("dom", "scen"), None),
            P(("dom", "scen")),
            P(("dom", "scen")),
            P(("dom", "scen"), None),
            P(("dom", "scen")),
            P(),
            P("scen", None),
            P(),
            P(),
            P("scen", None),
            P(),
        ),
        out_specs=P(("dom", "scen"), None),
        check_vma=False,
    )
```

profile of v0, /device:TPU:8, one launch (start us, length us, event | category | flops | bytes accessed | tf_op | source)
XLA Modules:
  0.0 204.4 jit_solution(11013594092646320890)
XLA Ops:
  6.5 0.0 copy-start
  6.5 0.0 copy-start.1
  6.5 0.0 all-gather.2.cloned.1.call-start
  6.5 0.7 all-gather.2.cloned.1.call-update
  7.3 0.7 compare_select_fusion
  8.0 0.1 copy.18
  8.1 0.1 reshape.46
  8.2 0.0 copy-done.1
  8.2 0.0 copy-start.6
  8.2 7.5 %gather_fusion.1 = bf16[2048,256]{1,0:T(8,128)(2,1)S(1)} fusion(bf16[2560,256]{1,0:T(8,128)(2,1)S(1)} %copy-done.1, s32[2048]{0:T(1024)S(1)} %broadcast_clamp_fusion), kind=kCustom, calls=%fused_computation.1 | custom fusion | bytes 2105344 | tf_op jit(solution)/shard_map/gather | solution.py:32
  15.7 0.0 copy-done.6
  15.7 0.0 copy-start.7
  15.7 0.1 iota_compare_fusion
  15.8 0.0 copy-start.5
  15.8 0.0 copy-start.4
  15.8 1.2 broadcast_select_fusion
  17.1 17.4 %all-to-all-start = ((bf16[128,16,256]{2,1,0:T(8,128)(2,1)}), bf16[128,16,256]{2,1,0:T(8,128)(2,1)S(1)}, u32[]{:S(2)}, u32[]{:S(2)}) async-start(bf16[128,16,256]{2,1,0:T(8,128)(2,1)} %broadcast_select_fusion), calls=%async_computation | async-start | bytes 2097152 | tf_op jit(solution)/shard_map/all_to_all | solution.py:34
  34.4 0.0 copy-done.7
  34.5 0.8 gather_fusion.3
  35.3 0.1 convert_select_fusion
  35.4 114.3 %all-reduce.1 = bf16[128,256]{1,0:T(8,128)(2,1)S(1)} all-reduce(f32[128,256]{1,0:T(8,128)S(1)} %convert_select_fusion), channel_id=1, replica_groups=mesh['dom'=128,'scen'=4] {'dom','scen'}, use_global_device_ids=true, to_apply=%region_0.1 | all-reduce | flops 32768 | bytes 196608 | tf_op jit(solution)/shard_map/psum | solution.py:42
  149.8 12.2 %all_gather.11 = bf16[256,256]{1,0:T(8,128)(2,1)S(1)} all-gather(bf16[64,256]{1,0:T(8,128)(2,1)} %param.26), channel_id=1, replica_groups=mesh['dom'=128,'scen'=4] {'scen'}, dimensions={0}, use_global_device_ids=true | all-gather | bytes 163840 | tf_op jit(solution)/shard_map/all_gather | solution.py:68
  162.0 0.0 copy-done.5
  162.0 13.2 %all_gather.10 = bf16[512,256]{1,0:T(8,128)(2,1)} all-gather(bf16[128,256]{1,0:T(8,128)(2,1)S(1)} %copy-done.5), channel_id=1, replica_groups=mesh['dom'=128,'scen'=4] {'scen'}, dimensions={0}, use_global_device_ids=true | all-gather | bytes 327680 | tf_op jit(solution)/shard_map/all_gather | solution.py:60
  175.1 0.7 compare_select_fusion.2
  175.8 0.7 compare_select_fusion.3
  176.4 0.6 pad_clamp_fusion.2
  177.0 0.0 copy-done.4
  177.0 2.7 %convolution_add_fusion.2 = f32[2560,256]{1,0:T(8,128)} fusion(bf16[16,2560]{1,0:T(8,128)(2,1)S(1)} %copy-done.4, bf16[16,256]{1,0:T(8,128)(2,1)} %param.24, f32[256]{0:T(256)} %param.25), kind=kOutput, calls=%fused_computation.6 | convolution fusion | flops 21626880 | bytes 2712576 | tf_op jit(solution)/shard_map/dot_general | solution.py:55
  179.8 0.0 all-to-all-done
  179.8 1.8 gather_fusion.2
  181.5 0.0 all-gather.2.cloned.1.call-done
  181.5 3.2 %gather_fusion = bf16[20,128,256]{2,1,0:T(8,128)(2,1)S(1)} fusion(bf16[80,128,256]{2,1,0:T(8,128)(2,1)} %bitcast.33, s32[1024]{0:T(1024)} %pad_clamp_fusion.2), kind=kCustom, calls=%fused_computation | custom fusion | bytes 2621520 | tf_op jit(solution)/shard_map/gather | solution.py:28
  184.8 0.0 copy-start.2
  184.8 0.0 copy-start.3
  184.8 1.7 fusion.52
  186.5 0.0 copy-done.2
  186.6 0.1 copy-done.3
  186.7 0.5 convolution_add_fusion.3
  187.2 0.0 copy-start.8
  187.2 0.0 copy-done
  187.2 0.5 fusion.1
  187.7 0.2 copy-done.8
  187.9 9.7 %fusion.2 = bf16[2560,256]{1,0:T(8,128)(2,1)} fusion(bf16[256,256]{1,0:T(8,128)(2,1)S(1)} %all_gather.11, bf16[2560,256]{1,0:T(8,128)(2,1)S(1)} %copy-done.1, f32[256]{0:T(256)S(1)} %copy-done.8, f32[2560,256]{1,0:T(8,128)} %convolution_add_fusion.2, bf16[512,256]{1,0:T(8,128)(2,1)} %all_gather.10, bf16[2560,256]{1,0:T(8,128)(2,1)S(1)} %fusion.1), kind=kOutput, calls=%fused_computation.11 | convolution fusion | flops 1057751040 | bytes 6947840 | tf_op jit(solution)/shard_map/dot_general | solution.py:66
  (5 shorter events, 0.0 us)
Async XLA Ops:
  6.5 180.7 %copy-start = (bf16[2560,128]{1,0:T(8,128)(2,1)S(1)}, bf16[2560,128]{1,0:T(8,128)(2,1)}, u32[]{:S(2)}) copy-start(bf16[2560,128]{1,0:T(8,128)(2,1)} %param.17) | copy-start | bytes 1966084
  6.5 1.6 copy-start.1
  6.5 175.0 %all-gather.2.cloned.1.call-start = ((), (), s32[]{:S(2)}) async-start(), calls=%async_computation.1 | async-start | bytes 6553600 | tf_op jit(solution)/shard_map/all_gather | solution.py:27
  8.2 7.5 %copy-start.6 = (s32[128]{0:T(128)S(1)}, s32[128]{0:T(128)}, u32[]{:S(2)}) copy-start(s32[128]{0:T(128)} %param.21) | copy-start | bytes 1540
  15.7 18.8 %copy-start.7 = (s32[128]{0:T(128)S(1)}, s32[128]{0:T(128)}, u32[]{:S(2)}) copy-start(s32[128]{0:T(128)} %param.22) | copy-start | bytes 1540
  15.8 146.2 %copy-start.5 = (bf16[128,256]{1,0:T(8,128)(2,1)S(1)}, bf16[128,256]{1,0:T(8,128)(2,1)}, u32[]{:S(2)}) copy-start(bf16[128,256]{1,0:T(8,128)(2,1)} %param.23) | copy-start | bytes 196612
  15.8 161.2 %copy-start.4 = (bf16[16,2560]{1,0:T(8,128)(2,1)S(1)}, bf16[16,2560]{1,0:T(8,128)(2,1)}, u32[]{:S(2)}) copy-start(bf16[16,2560]{1,0:T(8,128)(2,1)} %param.15) | copy-start | bytes 245764
  17.1 162.7 %all-to-all-start = ((bf16[128,16,256]{2,1,0:T(8,128)(2,1)}), bf16[128,16,256]{2,1,0:T(8,128)(2,1)S(1)}, u32[]{:S(2)}, u32[]{:S(2)}) async-start(bf16[128,16,256]{2,1,0:T(8,128)(2,1)} %broadcast_select_fusion), calls=%async_computation | async-start | bytes 2097152 | tf_op jit(solution)/shard_map/all_to_all | solution.py:34
  184.8 1.8 copy-start.2
  184.8 1.9 copy-start.3
  187.2 0.7 copy-start.8
Sparse Core Ops, SparseCore 0:
  9.5 66.8 all-gather.1
where the time goes:
time: 205 us; the launch traced here: 204 us
  blocking collectives  140 us (68%)
  starting transfers between devices  17.4 us (8%)
  matrix products  15.1 us (7%)
  local copies, waits for them, and re-layouts  13.9 us (7%)
  between operations  13.6 us (7%)
  other arithmetic  4.05 us (2%)
    psum x1, blocking collectives, per_device(): drivers = lax.psum(mine, ('dom', 'scen')).astype(jnp.bfloat16)  114 us
    all_to_all x1, starting transfers between devices, per_device(): lax.all_to_all(outgoing_rows, 'dom', split_axis=0, concat_axis=0, tiled=T...  17.4 us
    all_gather x1, blocking collectives, per_device(): lax.all_gather(first_weight, 'scen', axis=0, tiled=True)  13.2 us
    all_gather x1, blocking collectives, per_device(): lax.all_gather(second_weight, 'scen', axis=0, tiled=True)  12.2 us
    dot_general x1, matrix products, per_device(): jnp.dot(columns, lax.all_gather(second_weight, 'scen', axis=0, tiled=True...  9.68 us
    gather x1, local copies, waits for them, and re-layouts, per_device(): embedding[send_rows]  7.5 us
  transfers between devices with their start and end apart: 2, of which 0 were waited for; matrix products, arithmetic and copies ran while one was open for 8% of the time, Pallas kernels for 0%

commit v1 on v0

--- a/solution.py
+++ b/solution.py
@@ -55,10 +55,21 @@
         jnp.dot(scenario_feats.T, feature_weight, preferred_element_type=jnp.float32) + first_bias
     )
     columns = joined
+
+    def state_files(array_dim, dev_axis, local):
+        r_now = jnp.concatenate(
+            jax.lax.all_to_all(
+                jnp.stack(jax.lax.psum(1, axis_name=dev_axis) * [local]),
+                dev_axis,
+                split_axis=0,
+                concat_axis=0,
+            ),
+            axis=array_dim,
+        )
+        return r_now
+
     inner = starting + jnp.dot(
-        columns,
-        lax.all_gather(first_weight, "scen", axis=0, tiled=True),
-        preferred_element_type=jnp.float32,
+        columns, state_files(0, "scen", first_weight), preferred_element_type=jnp.float32
     )
     activated = jax.nn.gelu(inner, approximate=False).astype(jnp.bfloat16)
     residual = embedding.astype(jnp.float32) + second_bias

time: 205 us -> 198 us (0.966)
  the two profiles are of different devices: /device:TPU:8 before, /device:TPU:2 now
where the time goes in v1:
time: 198 us; the launch traced here: 197 us
  blocking collectives  126 us (64%)
  starting transfers between devices  23.1 us (12%)
  matrix products  15.1 us (8%)
  local copies, waits for them, and re-layouts  14.6 us (7%)
  between operations  13.6 us (7%)
  other arithmetic  4.06 us (2%)
    psum x1, blocking collectives, per_device(): drivers = lax.psum(mine, ('dom', 'scen')).astype(jnp.bfloat16)  115 us
    all_to_all x1, starting transfers between devices, per_device(): lax.all_to_all(outgoing_rows, 'dom', split_axis=0, concat_axis=0, tiled=T...  17.9 us
    all_gather x1, blocking collectives, per_device(): lax.all_gather(second_weight, 'scen', axis=0, tiled=True)  11 us
    dot_general x1, matrix products, per_device(): jnp.dot(columns, lax.all_gather(second_weight, 'scen', axis=0, tiled=True...  9.68 us
    gather x1, local copies, waits for them, and re-layouts, per_device(): embedding[send_rows]  7.5 us
    all_to_all x1, starting transfers between devices, state_files(): jax.lax.all_to_all(jnp.stack(jax.lax.psum(1, axis_name=dev_axis) * [local...  5.19 us
  transfers between devices with their start and end apart: 3, of which 0 were waited for; matrix products, arithmetic and copies ran while one was open for 12% of the time, Pallas kernels for 0%

profile of v1, /device:TPU:2, one launch (start us, length us, event | category | flops | bytes accessed | tf_op | source)
XLA Modules:
  0.0 197.1 jit_solution(6666367363958307642)
XLA Ops:
  6.5 0.0 copy-start
  6.5 0.0 copy-start.1
  6.5 0.0 all-gather.2.cloned.1.call-start
  6.5 0.7 all-gather.2.cloned.1.call-update
  7.3 0.7 compare_select_fusion
  8.0 0.1 copy.18
  8.1 0.1 reshape.52
  8.2 0.0 copy-done.1
  8.2 0.0 copy-start.6
  8.2 7.5 %gather_fusion.1 = bf16[2048,256]{1,0:T(8,128)(2,1)S(1)} fusion(bf16[2560,256]{1,0:T(8,128)(2,1)S(1)} %copy-done.1, s32[2048]{0:T(1024)S(1)} %broadcast_clamp_fusion), kind=kCustom, calls=%fused_computation.1 | custom fusion | bytes 2105344 | tf_op jit(solution)/shard_map/gather | solution.py:32
  15.7 0.0 copy-done.6
  15.7 0.0 copy-start.7
  15.7 0.1 iota_compare_fusion
  15.8 0.0 copy-start.4
  15.8 1.2 broadcast_select_fusion
  17.0 0.0 copy-start.5
  17.0 17.9 %all-to-all-start = ((bf16[128,16,256]{2,1,0:T(8,128)(2,1)}), bf16[128,16,256]{2,1,0:T(8,128)(2,1)S(1)}, u32[]{:S(2)}, u32[]{:S(2)}) async-start(bf16[128,16,256]{2,1,0:T(8,128)(2,1)} %broadcast_select_fusion), calls=%async_computation | async-start | bytes 2097152 | tf_op jit(solution)/shard_map/all_to_all | solution.py:34
  35.0 0.0 copy-done.7
  35.1 0.8 gather_fusion.3
  35.9 0.1 convert_select_fusion
  36.0 114.9 %all-reduce.1 = bf16[128,256]{1,0:T(8,128)(2,1)S(1)} all-reduce(f32[128,256]{1,0:T(8,128)S(1)} %convert_select_fusion), channel_id=1, replica_groups=mesh['dom'=128,'scen'=4] {'dom','scen'}, use_global_device_ids=true, to_apply=%region_0.1 | all-reduce | flops 32768 | bytes 196608 | tf_op jit(solution)/shard_map/psum | solution.py:42
  150.9 11.0 %all_gather.7 = bf16[256,256]{1,0:T(8,128)(2,1)S(1)} all-gather(bf16[64,256]{1,0:T(8,128)(2,1)} %param.26), channel_id=1, replica_groups=mesh['dom'=128,'scen'=4] {'scen'}, dimensions={0}, use_global_device_ids=true | all-gather | bytes 163840 | tf_op jit(solution)/shard_map/all_gather | solution.py:79
  161.9 0.7 compare_select_fusion.2
  162.6 0.7 compare_select_fusion.3
  163.2 0.6 pad_clamp_fusion.2
  163.8 0.0 copy-done.4
  163.8 2.7 %convolution_add_fusion.2 = f32[2560,256]{1,0:T(8,128)} fusion(bf16[16,2560]{1,0:T(8,128)(2,1)S(1)} %copy-done.4, bf16[16,256]{1,0:T(8,128)(2,1)} %param.24, f32[256]{0:T(256)} %param.25), kind=kOutput, calls=%fused_computation.6 | convolution fusion | flops 21626880 | bytes 2712576 | tf_op jit(solution)/shard_map/dot_general | solution.py:55
  166.6 0.0 all-to-all-done
  166.6 0.0 copy-done.5
  166.6 0.7 stack.2
  167.3 5.2 %all-to-all-start.1 = ((bf16[4,128,256]{2,1,0:T(8,128)(2,1)}), bf16[4,128,256]{2,1,0:T(8,128)(2,1)}, u32[]{:S(2)}, u32[]{:S(2)}) async-start(bf16[4,128,256]{2,1,0:T(8,128)(2,1)} %stack.2), calls=%async_computation.1 | async-start | bytes 524288 | tf_op jit(solution)/shard_map/all_to_all | solution.py:61
  172.5 1.8 gather_fusion.2
  174.3 0.0 all-gather.2.cloned.1.call-done
  174.3 3.2 %gather_fusion = bf16[20,128,256]{2,1,0:T(8,128)(2,1)S(1)} fusion(bf16[80,128,256]{2,1,0:T(8,128)(2,1)} %bitcast.34, s32[1024]{0:T(1024)} %pad_clamp_fusion.2), kind=kCustom, calls=%fused_computation | custom fusion | bytes 2621520 | tf_op jit(solution)/shard_map/gather | solution.py:28
  177.5 0.0 copy-start.2
  177.5 0.0 copy-start.3
  177.5 1.7 fusion.52
  179.3 0.0 copy-done.2
  179.3 0.1 copy-done.3
  179.4 0.5 convolution_add_fusion.3
  179.9 0.0 copy-start.8
  179.9 0.0 copy-done
  179.9 0.5 fusion.1
  180.4 0.0 all-to-all-done.1
  180.5 0.2 copy-done.8
  180.6 9.7 %fusion.2 = bf16[2560,256]{1,0:T(8,128)(2,1)} fusion(bf16[256,256]{1,0:T(8,128)(2,1)S(1)} %all_gather.7, bf16[2560,256]{1,0:T(8,128)(2,1)S(1)} %copy-done.1, f32[256]{0:T(256)S(1)} %copy-done.8, f32[2560,256]{1,0:T(8,128)} %convolution_add_fusion.2, bf16[512,256]{1,0:T(8,128)(2,1)} %bitcast.8, bf16[2560,256]{1,0:T(8,128)(2,1)S(1)} %fusion.1), kind=kOutput, calls=%fused_computation.11 | convolution fusion | flops 1057751040 | bytes 6947840 | tf_op jit(solution)/shard_map/dot_general | solution.py:77
  (5 shorter events, 0.0 us)
Async XLA Ops:
  6.5 173.4 %copy-start = (bf16[2560,128]{1,0:T(8,128)(2,1)S(1)}, bf16[2560,128]{1,0:T(8,128)(2,1)}, u32[]{:S(2)}) copy-start(bf16[2560,128]{1,0:T(8,128)(2,1)} %param.17) | copy-start | bytes 1966084
  6.5 1.6 copy-start.1
  6.5 167.7 %all-gather.2.cloned.1.call-start = ((), (), s32[]{:S(2)}) async-start(), calls=%async_computation.2 | async-start | bytes 6553600 | tf_op jit(solution)/shard_map/all_gather | solution.py:27
  8.2 7.5 %copy-start.6 = (s32[128]{0:T(128)S(1)}, s32[128]{0:T(128)}, u32[]{:S(2)}) copy-start(s32[128]{0:T(128)} %param.21) | copy-start | bytes 1540
  15.7 19.3 %copy-start.7 = (s32[128]{0:T(128)S(1)}, s32[128]{0:T(128)}, u32[]{:S(2)}) copy-start(s32[128]{0:T(128)} %param.22) | copy-start | bytes 1540
  15.8 148.1 %copy-start.4 = (bf16[16,2560]{1,0:T(8,128)(2,1)S(1)}, bf16[16,2560]{1,0:T(8,128)(2,1)}, u32[]{:S(2)}) copy-start(bf16[16,2560]{1,0:T(8,128)(2,1)} %param.15) | copy-start | bytes 245764
  17.0 149.5 %copy-start.5 = (bf16[128,256]{1,0:T(8,128)(2,1)S(1)}, bf16[128,256]{1,0:T(8,128)(2,1)}, u32[]{:S(2)}) copy-start(bf16[128,256]{1,0:T(8,128)(2,1)} %param.23) | copy-start | bytes 196612
  17.0 149.5 %all-to-all-start = ((bf16[128,16,256]{2,1,0:T(8,128)(2,1)}), bf16[128,16,256]{2,1,0:T(8,128)(2,1)S(1)}, u32[]{:S(2)}, u32[]{:S(2)}) async-start(bf16[128,16,256]{2,1,0:T(8,128)(2,1)} %broadcast_select_fusion), calls=%async_computation | async-start | bytes 2097152 | tf_op jit(solution)/shard_map/all_to_all | solution.py:34
  167.3 13.1 %all-to-all-start.1 = ((bf16[4,128,256]{2,1,0:T(8,128)(2,1)}), bf16[4,128,256]{2,1,0:T(8,128)(2,1)}, u32[]{:S(2)}, u32[]{:S(2)}) async-start(bf16[4,128,256]{2,1,0:T(8,128)(2,1)} %stack.2), calls=%async_computation.1 | async-start | bytes 524288 | tf_op jit(solution)/shard_map/all_to_all | solution.py:61
  177.5 1.8 copy-start.2
  177.5 1.9 copy-start.3
  179.9 0.7 copy-start.8
Sparse Core Ops, SparseCore 0:
  9.5 66.4 all-gather.1
